TPU v7x, 32 devices: a whole 2x2x4 slice. The times are simulated.
32 devices in a mesh: wide: 2 (over core), op: 16 (over z, y, x).
Axes of the slice: x: 2, y: 2, z: 4, core: 2. Of those that a mesh axis runs over, the one named last changes fastest.
Arguments:
- wavefunction: bfloat16 [32, 4, 512, 512], P('wide', None, 'op'), may hold values from -6 to 6
- left_ops: bfloat16 [128, 512, 512], P(('wide', 'op')), may hold values from -0.0390625 to 0.0390625
- right_ops: bfloat16 [128, 512, 512], P(('wide', 'op')), may hold values from -0.25 to 0.25
- in_sector: int32 [128], P(('wide', 'op')), may hold values from 0 to 31
- live_count: int32 [32], P(('wide', 'op')), may hold values from 2 to 4, as said below
Outputs:
- sigma_blocks: bfloat16 [2, 4, 512, 512], P('wide', None, 'op')
Inputs may be any that keep to these rules, and one draw needn't show every extreme that they name: `live_count`: in each aligned group of 16 entries (the devices of one op group), entries i and i + 8 sum to 6, and exactly 4 entries are 4.
All inputs are finite; a program needn't handle non-finite values.
Results may differ from a plain program's by a relative error of at most 0.0065.
Values may be sent and summed in bfloat16 or wider, within the bound.
A program may use at most 64 MiB of HBM per device.

v0:
```python
import jax
import jax.numpy as jnp
from jax import lax
from jax.sharding import PartitionSpec as P


def from_behind(x, axis, by):
    devices = lax.axis_size(axis)
    return lax.ppermute(x, axis, [(i, (i + by) % devices) for i in range(devices)])


def sandwich(sector, left_op, right_op):
    half_step = jnp.einsum(
        "smk,nk->smn", sector, right_op, preferred_element_type=jnp.float32
    ).astype(jnp.bfloat16)
    return jnp.einsum("im,smn->sin", left_op, half_step, preferred_element_type=jnp.float32)


def local(wavefunction, left_ops, right_ops, in_sector, live_count):
    group_size = lax.axis_size("op")
    slot_count = left_ops.shape[0]
    ins_all, live_all = (
        lax.all_gather(in_sector, "op", axis=0, tiled=True),
        lax.all_gather(live_count, "op", axis=0, tiled=True),
    )
    ins_grid = ins_all.reshape(group_size, slot_count)
    my_live = live_count[0]
    rows_all = lax.all_gather(wavefunction, "wide", axis=0, tiled=True)
    partner_ins = jnp.roll(ins_grid[:, slot_count - 1], group_size // 2)
    third_in = jnp.where(live_all >= 3, ins_grid[:, 2], partner_ins)
    work_grid = jnp.concatenate([ins_grid[:, :2], third_in[:, None]], axis=1)
    arrived_left, arrived_right = from_behind(
        (left_ops[slot_count - 1], right_ops[slot_count - 1]), "op", group_size // 2
    )
    own_third = my_live >= 3
    work_left = jnp.stack(
        [left_ops[0], left_ops[1], jnp.where(own_third, left_ops[2], arrived_left)]
    )
    work_right = jnp.stack(
        [right_ops[0], right_ops[1], jnp.where(own_third, right_ops[2], arrived_right)]
    )
    weights = [jnp.float32(1.0) for slot_index in range(slot_count - 1)]
    work_count = work_grid.shape[1]
    outgoing = jnp.take(rows_all, work_grid.reshape(-1), axis=0)
    arrived = lax.all_to_all(outgoing, "op", split_axis=0, concat_axis=2, tiled=True)
    partial_value = jnp.zeros(arrived.shape[1:], jnp.float32)
    for slot_index in range(work_count):
        partial_value = partial_value + weights[slot_index] * sandwich(
            arrived[slot_index], work_left[slot_index], work_right[slot_index]
        )
    summed = lax.psum_scatter(partial_value[None], "op", scatter_dimension=2, tiled=True)
    return summed.astype(jnp.bfloat16)


def solution(mesh):
    placed = (
        P("wide", None, "op", None),
        P(("wide", "op"), None, None),
        P(("wide", "op"), None, None),
        P(("wide", "op")),
        P(("wide", "op")),
    )
    return jax.shard_map(
        local, mesh=mesh, in_specs=placed, out_specs=P("wide", None, "op", None), check_vma=False
    )
```

profile of v0, /device:TPU:0, one launch (start us, length us, event | category | flops | bytes accessed | tf_op | source)
XLA Modules:
  0.0 432.0 jit_solution(4435426553336007252)
XLA Ops:
  6.5 0.0 copy-start.1
  6.5 0.0 copy-start.2
  6.5 0.0 all-gather.2.cloned.1.call-start
  6.5 0.7 all-gather.2.cloned.1.call-update
  7.9 0.0 copy-done.1
  7.9 0.6 fusion.34
  9.2 0.7 dynamic-update-slice.1
  9.9 0.0 copy-done.2
  9.9 0.2 dynamic-update-slice
  10.1 16.2 %all-reduce.3 = (s32[64]{0:T(128)S(1)}, s32[16]{0:T(128)S(1)}) all-reduce(s32[64]{0:T(128)S(1)} %dynamic-update-slice, s32[16]{0:T(128)S(1)} %dynamic-update-slice.1), channel_id=1, replica_groups=mesh['wide'=2,'op'=16] {'op'}, use_global_device_ids=true, to_apply=%add | all-reduce | flops 80 | bytes 640
  26.3 0.1 reshape.52
  26.4 0.2 slice_reduce_fusion.2
  26.6 0.2 slice_reduce_fusion
  26.8 0.1 fusion.31
  26.9 0.1 copy.29
  27.0 0.1 pad_add_fusion
  27.0 0.1 reshape.54
  27.1 0.1 reshape.53
  27.3 0.0 all-gather.2.cloned.1.call-done
  27.3 7.1 %gather_fusion = bf16[48,4,32,512]{3,2,1,0:T(8,128)(2,1)} fusion(bf16[32,4,32,512]{3,2,1,0:T(8,128)(2,1)} %all-gather.2.cloned.1.call-done, s32[1024]{0:T(1024)S(1)} %pad_clamp_fusion), kind=kCustom, calls=%fused_computation | custom fusion | bytes 12583104 | tf_op jit(solution)/shard_map/jit(_take)/gather | solution.py:44
  34.5 6.1 %broadcast_select_fusion = bf16[48,4,32,512]{3,2,1,0:T(8,128)(2,1)} fusion(bf16[48,4,32,512]{3,2,1,0:T(8,128)(2,1)} %gather_fusion, pred[48]{0:T(512)(128)(4,1)S(1)} %compare_and_fusion), kind=kLoop, calls=%fused_computation.1 | loop fusion | flops 3145728 | bytes 12582960 | tf_op jit(solution)/shard_map/jit(_take)/select_n | solution.py:44
  40.6 4.8 %all-to-all-start = ((bf16[48,4,32,512]{3,2,1,0:T(8,128)(2,1)}), bf16[48,4,32,512]{3,2,1,0:T(8,128)(2,1)}, u32[]{:S(2)}, u32[]{:S(2)}) async-start(bf16[48,4,32,512]{3,2,1,0:T(8,128)(2,1)} %broadcast_select_fusion), calls=%async_computation | async-start | bytes 12582912 | tf_op jit(solution)/shard_map/all_to_all | solution.py:45
  45.4 1.9 slice_bitcast_fusion.1
  47.3 2.8 collective-permute-start
  50.1 1.9 slice_bitcast_fusion
  52.0 0.1 collective-permute-start.1
  52.8 134.8 %all-to-all-done = bf16[48,4,32,512]{3,2,1,0:T(8,128)(2,1)} async-done(((bf16[48,4,32,512]{3,2,1,0:T(8,128)(2,1)}), bf16[48,4,32,512]{3,2,1,0:T(8,128)(2,1)}, u32[]{:S(2)}, u32[]{:S(2)}) %all-to-all-start) | async-done | bytes 6291488 | tf_op jit(solution)/shard_map/all_to_all | solution.py:45
  187.7 5.1 %fusion.33 = (bf16[1,4,16,32,512]{4,3,1,0,2:T(8,128)(2,1)}, bf16[1,4,16,32,512]{4,3,1,0,2:T(8,128)(2,1)S(1)}, bf16[1,4,16,32,512]{4,3,1,0,2:T(8,128)(2,1)S(1)}) fusion(bf16[3,4,16,32,512]{4,3,1,0,2:T(8,128)(2,1)} %bitcast.5), kind=kLoop, calls=%fused_computation.40 | loop fusion | bytes 12582912 | tf_op jit(solution)/shard_map/slice | solution.py:49
  192.8 1.6 copy.32
  194.4 6.1 %fusion.1 = f32[4,512,512]{2,1,0:T(8,128)} fusion(bf16[4,512,512]{2,1,0:T(8,128)(2,1)} %bitcast.64, bf16[4,512,512]{2,1,0:T(8,128)(2,1)} %param.6, bf16[4,512,512]{2,1,0:T(8,128)(2,1)} %param.7), kind=kOutput, calls=%fused_computation.4 | convolution fusion | flops 2148532224 | bytes 7340032 | tf_op jit(solution)/shard_map/im,smn->sin/dot_general | solution.py:16
  200.5 0.0 copy-start
  200.5 1.5 copy.30
  202.0 0.8 copy-done
  202.9 0.2 copy.34
  203.1 6.2 %fusion.3 = f32[4,512,512]{2,1,0:T(8,128)} fusion(bf16[4,512,512]{2,1,0:T(8,128)(2,1)} %bitcast.63, bf16[4,512,512]{2,1,0:T(8,128)(2,1)} %param.6, bf16[4,512,512]{2,1,0:T(8,128)(2,1)} %param.7), kind=kOutput, calls=%fused_computation.6 | convolution fusion | flops 2148532224 | bytes 7340032 | tf_op jit(solution)/shard_map/im,smn->sin/dot_general | solution.py:16
  209.3 9.3 %collective-permute-done = bf16[512,512]{1,0:T(8,128)(2,1)S(1)} collective-permute-done((bf16[512,512]{1,0:T(8,128)(2,1)}, bf16[512,512]{1,0:T(8,128)(2,1)S(1)}, u32[]{:S(2)}, u32[]{:S(2)}) %collective-permute-start) | collective-permute-done | bytes 524320 | tf_op jit(solution)/shard_map/ppermute | solution.py:9
  218.5 10.3 %collective-permute-done.1 = bf16[512,512]{1,0:T(8,128)(2,1)S(1)} collective-permute-done((bf16[512,512]{1,0:T(8,128)(2,1)}, bf16[512,512]{1,0:T(8,128)(2,1)S(1)}, u32[]{:S(2)}, u32[]{:S(2)}) %collective-permute-start.1) | collective-permute-done | bytes 524320 | tf_op jit(solution)/shard_map/ppermute | solution.py:9
  228.8 8.2 %add_bitcast_fusion = f32[1,4,512,512]{2,3,1,0:T(8,128)} fusion(f32[4,512,512]{2,1,0:T(8,128)} %fusion.3, f32[4,512,512]{2,1,0:T(8,128)} %fusion.1, bf16[4,512,512]{2,1,0:T(8,128)(2,1)S(1)} %bitcast.62, bf16[512,512]{1,0:T(8,128)(2,1)S(1)} %collective-permute-done.1, bf16[512,512]{1,0:T(8,128)(2,1)S(1)} %collective-permute-done, ...), kind=kOutput, calls=%fused_computation.2 | convolution fusion | flops 2151153664 | bytes 16778240 | tf_op jit(solution)/shard_map/im,smn->sin/dot_general | solution.py:16
  237.0 5.4 %copy.36 = f32[1,4,512,512]{3,1,0,2:T(4,128)} copy(f32[1,4,512,512]{2,3,1,0:T(8,128)} %add_bitcast_fusion) | data formatting | bytes 8388608 | tf_op jit(solution)/shard_map/broadcast_in_dim | solution.py:51
  242.4 182.0 %all-reduce.5 = bf16[1,4,512,512]{3,1,0,2:T(4,128)(2,1)S(1)} all-reduce(f32[1,4,512,512]{3,1,0,2:T(4,128)} %copy.36), channel_id=2, replica_groups=mesh['wide'=2,'op'=16] {'op'}, use_global_device_ids=true, to_apply=%region_0.1.clone | all-reduce | flops 1048576 | bytes 6291456
  424.5 0.1 dynamic-slice_convert_fusion
  424.5 0.7 copy.37
  (5 shorter events, 0.0 us)
Async XLA Ops:
  6.5 1.4 copy-start.1
  6.5 3.3 copy-start.2
  6.5 20.8 %all-gather.2.cloned.1.call-start = ((), (), s32[]{:S(2)}) async-start(), calls=%async_computation.1 | async-start | bytes 6291456 | tf_op jit(solution)/shard_map/all_gather | solution.py:28
  40.6 147.1 %all-to-all-start = ((bf16[48,4,32,512]{3,2,1,0:T(8,128)(2,1)}), bf16[48,4,32,512]{3,2,1,0:T(8,128)(2,1)}, u32[]{:S(2)}, u32[]{:S(2)}) async-start(bf16[48,4,32,512]{3,2,1,0:T(8,128)(2,1)} %broadcast_select_fusion), calls=%async_computation | async-start | bytes 12582912 | tf_op jit(solution)/shard_map/all_to_all | solution.py:45
  47.3 171.2 %collective-permute-start = (bf16[512,512]{1,0:T(8,128)(2,1)}, bf16[512,512]{1,0:T(8,128)(2,1)S(1)}, u32[]{:S(2)}, u32[]{:S(2)}) collective-permute-start(bf16[512,512]{1,0:T(8,128)(2,1)} %slice_bitcast_fusion.1), channel_id=1, source_target_pairs={{0,8},{1,9},{2,10},{3,11},{4,12},{5,13},{6,14},{7,15},{8,0},{9,1},... | collective-permute-start | bytes 1572872 | tf_op jit(solution)/shard_map/ppermute | solution.py:9
  52.0 176.8 %collective-permute-start.1 = (bf16[512,512]{1,0:T(8,128)(2,1)}, bf16[512,512]{1,0:T(8,128)(2,1)S(1)}, u32[]{:S(2)}, u32[]{:S(2)}) collective-permute-start(bf16[512,512]{1,0:T(8,128)(2,1)} %slice_bitcast_fusion), channel_id=1, source_target_pairs={{0,8},{1,9},{2,10},{3,11},{4,12},{5,13},{6,14},{7,15},{8,0},{9,1},... | collective-permute-start | bytes 1572872 | tf_op jit(solution)/shard_map/ppermute | solution.py:9
  200.5 2.3 copy-start
Sparse Core Ops, SparseCore 0:
  8.9 16.3 all-gather.1
where the time goes:
time: 433 us; the launch traced here: 432 us
  blocking collectives  198 us (46%)
  waiting for transfers between devices  155 us (36%)
  local copies, waits for them, and re-layouts  28.8 us (7%)
  matrix products  20.5 us (5%)
  between operations  15.4 us (4%)
  starting transfers between devices  7.76 us (2%)
  other arithmetic  6.28 us (1%)
    unnamed x2, blocking collectives  198 us
    all_to_all x1, waiting for transfers between devices, local(): lax.all_to_all(outgoing, 'op', split_axis=0, concat_axis=2, tiled=True)  135 us
    dot_general x3, matrix products, sandwich(): jnp.einsum('im,smn->sin', left_op, half_step, preferred_element_type=jnp....  20.5 us
    ppermute x2, waiting for transfers between devices, from_behind(): lax.ppermute(x, axis, [(i, (i + by) % devices) for i in range(devices)])  19.5 us
  transfers between devices with their start and end apart: 4, of which 3 were waited for; matrix products, arithmetic and copies ran while one was open for 6% of the time, Pallas kernels for 0%

commit v1 on v0

--- a/solution.py
+++ b/solution.py
@@ -42,7 +42,10 @@
     weights = [jnp.float32(1.0) for slot_index in range(slot_count - 1)]
     work_count = work_grid.shape[1]
     outgoing = jnp.take(rows_all, work_grid.reshape(-1), axis=0)
-    arrived = lax.all_to_all(outgoing, "op", split_axis=0, concat_axis=2, tiled=True)
+    count = lax.axis_size("op")
+    blocks = jnp.stack(jnp.split(outgoing, count, axis=0), axis=0)
+    blocks = lax.all_to_all(blocks, "op", split_axis=0, concat_axis=0)
+    arrived = jnp.concatenate(blocks, axis=2)
     partial_value = jnp.zeros(arrived.shape[1:], jnp.float32)
     for slot_index in range(work_count):
         partial_value = partial_value + weights[slot_index] * sandwich(

time: 433 us -> 441 us (1.018)
  local copies, waits for them, and re-layouts: 28.8 us -> 40 us
    unnamed x11 -> x20, local copies, waits for them, and re-layouts: 2.38 us -> 14.9 us
    slice x4 -> x1, local copies, waits for them, and re-layouts: 8.5 us -> 2.83 us  [local(): arrived[slot_index]]
    ppermute x2, waiting for transfers between devices: 19.5 us -> 24.8 us  [from_behind(): lax.ppermute(x, axis, [(i, (i + by) % devices) for i in range(devices)])]
where the time goes in v1:
time: 441 us; the launch traced here: 440 us
  blocking collectives  196 us (44%)
  waiting for transfers between devices  157 us (36%)
  local copies, waits for them, and re-layouts  40 us (9%)
  matrix products  20.5 us (5%)
  between operations  15.5 us (4%)
  starting transfers between devices  7.73 us (2%)
    unnamed x2, blocking collectives  196 us
    all_to_all x1, waiting for transfers between devices, local(): blocks = lax.all_to_all(blocks, 'op', split_axis=0, concat_axis=0)  131 us
    ppermute x2, waiting for transfers between devices, from_behind(): lax.ppermute(x, axis, [(i, (i + by) % devices) for i in range(devices)])  24.8 us
    dot_general x3, matrix products, sandwich(): jnp.einsum('im,smn->sin', left_op, half_step, preferred_element_type=jnp....  20.5 us
    unnamed x20, local copies, waits for them, and re-layouts  14.9 us
  transfers between devices with their start and end apart: 4, of which 3 were waited for; matrix products, arithmetic and copies ran while one was open for 6% of the time, Pallas kernels for 0%

profile of v1, /device:TPU:0, one launch (start us, length us, event | category | flops | bytes accessed | tf_op | source)
XLA Modules:
  0.0 439.9 jit_solution(6822524393503768499)
XLA Ops:
  6.5 0.7 all-gather.2.cloned.1.call-update
  7.9 1.4 fusion.50
  10.0 0.8 dynamic-update-slice.1
  10.8 0.8 dynamic-update-slice
  11.7 16.2 %all-reduce.3 = (s32[64]{0:T(128)S(1)}, s32[16]{0:T(128)S(1)}) all-reduce(s32[64]{0:T(128)S(1)} %dynamic-update-slice, s32[16]{0:T(128)S(1)} %dynamic-update-slice.1), channel_id=1, replica_groups=mesh['wide'=2,'op'=16] {'op'}, use_global_device_ids=true, to_apply=%add | all-reduce | flops 80 | bytes 640
  27.9 0.1 reshape.56
  27.9 0.2 slice_reduce_fusion.2
  28.2 0.2 slice_reduce_fusion
  28.3 0.1 fusion.47
  28.4 0.1 copy.34
  28.5 0.1 pad_add_fusion
  28.6 0.1 reshape.58
  28.7 0.1 reshape.57
  28.8 7.2 %gather_fusion = bf16[48,4,32,512]{3,2,1,0:T(8,128)(2,1)} fusion(bf16[32,4,32,512]{3,2,1,0:T(8,128)(2,1)} %all-gather.2.cloned.1.call-done, s32[1024]{0:T(1024)S(1)} %pad_clamp_fusion), kind=kCustom, calls=%fused_computation | custom fusion | bytes 12583104 | tf_op jit(solution)/shard_map/jit(_take)/gather | solution.py:44
  36.0 3.4 broadcast_select_fusion
  39.5 0.8 fusion.46
  40.3 0.8 fusion.45
  41.1 0.8 fusion.44
  41.8 0.8 fusion.43
  42.6 0.8 fusion.42
  43.4 0.8 fusion.41
  44.2 0.8 fusion.40
  45.0 0.8 fusion.39
  45.9 0.8 fusion.38
  46.6 0.8 fusion.37
  47.4 0.8 fusion.36
  48.2 0.8 fusion.35
  49.0 0.8 fusion.34
  49.8 0.8 fusion.33
  50.6 0.8 fusion.32
  51.4 0.8 fusion.31
  52.1 4.8 %all-to-all-start = ((bf16[16,3,4,32,512]{4,3,2,1,0:T(8,128)(2,1)}), bf16[16,3,4,32,512]{4,3,2,1,0:T(8,128)(2,1)}, u32[]{:S(2)}, u32[]{:S(2)}) async-start(bf16[16,3,4,32,512]{4,3,2,1,0:T(8,128)(2,1)} %fusion.31), calls=%async_computation | async-start | bytes 12582912 | tf_op jit(solution)/shard_map/all_to_all | solution.py:47
  57.0 1.9 slice_bitcast_fusion.1
  58.9 2.5 collective-permute-start
  61.4 1.9 slice_bitcast_fusion
  63.3 0.4 collective-permute-start.1
  64.4 131.0 %all-to-all-done = bf16[16,3,4,32,512]{4,3,2,1,0:T(8,128)(2,1)} async-done(((bf16[16,3,4,32,512]{4,3,2,1,0:T(8,128)(2,1)}), bf16[16,3,4,32,512]{4,3,2,1,0:T(8,128)(2,1)}, u32[]{:S(2)}, u32[]{:S(2)}) %all-to-all-start) | async-done | bytes 6291488 | tf_op jit(solution)/shard_map/all_to_all | solution.py:47
  195.4 3.6 copy.45
  198.9 2.8 fusion.49
  201.8 6.1 %fusion.1 = f32[4,512,512]{2,1,0:T(8,128)} fusion(bf16[4,512,512]{2,1,0:T(8,128)(2,1)} %bitcast.129, bf16[4,512,512]{2,1,0:T(8,128)(2,1)} %param.6, bf16[4,512,512]{2,1,0:T(8,128)(2,1)} %param.7), kind=kOutput, calls=%fused_computation.5 | convolution fusion | flops 2148532224 | bytes 7340032 | tf_op jit(solution)/shard_map/im,smn->sin/dot_general | solution.py:16
  207.9 6.2 %fusion.3 = f32[4,512,512]{2,1,0:T(8,128)} fusion(bf16[4,512,512]{2,1,0:T(8,128)(2,1)} %bitcast.128, bf16[4,512,512]{2,1,0:T(8,128)(2,1)} %param.6, bf16[4,512,512]{2,1,0:T(8,128)(2,1)} %param.7), kind=kOutput, calls=%fused_computation.7 | convolution fusion | flops 2148532224 | bytes 7340032 | tf_op jit(solution)/shard_map/im,smn->sin/dot_general | solution.py:16
  214.1 14.6 %collective-permute-done = bf16[512,512]{1,0:T(8,128)(2,1)S(1)} collective-permute-done((bf16[512,512]{1,0:T(8,128)(2,1)}, bf16[512,512]{1,0:T(8,128)(2,1)S(1)}, u32[]{:S(2)}, u32[]{:S(2)}) %collective-permute-start) | collective-permute-done | bytes 524320 | tf_op jit(solution)/shard_map/ppermute | solution.py:9
  228.6 10.2 %collective-permute-done.1 = bf16[512,512]{1,0:T(8,128)(2,1)S(1)} collective-permute-done((bf16[512,512]{1,0:T(8,128)(2,1)}, bf16[512,512]{1,0:T(8,128)(2,1)S(1)}, u32[]{:S(2)}, u32[]{:S(2)}) %collective-permute-start.1) | collective-permute-done | bytes 524320 | tf_op jit(solution)/shard_map/ppermute | solution.py:9
  238.9 8.2 %add_bitcast_fusion = f32[1,4,512,512]{2,3,1,0:T(8,128)} fusion(f32[4,512,512]{2,1,0:T(8,128)} %fusion.3, f32[4,512,512]{2,1,0:T(8,128)} %fusion.1, bf16[4,512,512]{2,1,0:T(8,128)(2,1)S(1)} %bitcast.127, bf16[512,512]{1,0:T(8,128)(2,1)S(1)} %collective-permute-done.1, bf16[512,512]{1,0:T(8,128)(2,1)S(1)} %collective-permute-done, ...), kind=kOutput, calls=%fused_computation.3 | convolution fusion | flops 2151153664 | bytes 16778240 | tf_op jit(solution)/shard_map/im,smn->sin/dot_general | solution.py:16
  247.0 5.4 %copy.39 = f32[1,4,512,512]{3,1,0,2:T(4,128)} copy(f32[1,4,512,512]{2,3,1,0:T(8,128)} %add_bitcast_fusion) | data formatting | bytes 8388608 | tf_op jit(solution)/shard_map/broadcast_in_dim | solution.py:54
  252.5 179.8 %all-reduce.5 = bf16[1,4,512,512]{3,1,0,2:T(4,128)(2,1)S(1)} all-reduce(f32[1,4,512,512]{3,1,0,2:T(4,128)} %copy.39), channel_id=2, replica_groups=mesh['wide'=2,'op'=16] {'op'}, use_global_device_ids=true, to_apply=%region_0.1.clone | all-reduce | flops 1048576 | bytes 6291456
  432.3 0.1 dynamic-slice_convert_fusion
  432.4 0.7 copy.40
  (7 shorter events, 0.0 us)
Async XLA Ops:
  6.5 22.3 %all-gather.2.cloned.1.call-start = ((), (), s32[]{:S(2)}) async-start(), calls=%async_computation.1 | async-start | bytes 6291456 | tf_op jit(solution)/shard_map/all_gather | solution.py:28
  52.1 143.2 %all-to-all-start = ((bf16[16,3,4,32,512]{4,3,2,1,0:T(8,128)(2,1)}), bf16[16,3,4,32,512]{4,3,2,1,0:T(8,128)(2,1)}, u32[]{:S(2)}, u32[]{:S(2)}) async-start(bf16[16,3,4,32,512]{4,3,2,1,0:T(8,128)(2,1)} %fusion.31), calls=%async_computation | async-start | bytes 12582912 | tf_op jit(solution)/shard_map/all_to_all | solution.py:47
  58.9 169.7 %collective-permute-start = (bf16[512,512]{1,0:T(8,128)(2,1)}, bf16[512,512]{1,0:T(8,128)(2,1)S(1)}, u32[]{:S(2)}, u32[]{:S(2)}) collective-permute-start(bf16[512,512]{1,0:T(8,128)(2,1)} %slice_bitcast_fusion.1), channel_id=1, source_target_pairs={{0,8},{1,9},{2,10},{3,11},{4,12},{5,13},{6,14},{7,15},{8,0},{9,1},... | collective-permute-start | bytes 1572872 | tf_op jit(solution)/shard_map/ppermute | solution.py:9
  63.3 175.6 %collective-permute-start.1 = (bf16[512,512]{1,0:T(8,128)(2,1)}, bf16[512,512]{1,0:T(8,128)(2,1)S(1)}, u32[]{:S(2)}, u32[]{:S(2)}) collective-permute-start(bf16[512,512]{1,0:T(8,128)(2,1)} %slice_bitcast_fusion), channel_id=1, source_target_pairs={{0,8},{1,9},{2,10},{3,11},{4,12},{5,13},{6,14},{7,15},{8,0},{9,1},... | collective-permute-start | bytes 1572872 | tf_op jit(solution)/shard_map/ppermute | solution.py:9
Sparse Core Ops, SparseCore 0:
  8.9 16.3 all-gather.1
